TPU v7x, 32 devices: a whole 2x2x4 slice. The times are simulated.
32 devices in a mesh: row: 16 (over z, y, x), col: 2 (over core).
Axes of the slice: x: 2, y: 2, z: 4, core: 2. Of those that a mesh axis runs over, the one named last changes fastest.
Arguments:
- features: bfloat16 [8192, 128], P(('row', 'col')), may hold values from -6 to 6
- weight: bfloat16 [128, 256], replicated, may hold values from -0.5 to 0.5
- bias: float32 [256], replicated, may hold values from -3 to 3
- grad_out: bfloat16 [8192, 256], P(('row', 'col')), may hold values from -6 to 6
- tiles: bfloat16 [32, 128, 128, 128], P(('row', 'col')), may hold values from -0.25 to 0.25
- tile_count: int32 [32], P(('row', 'col')), may hold values from 1 to 128, as said below
- tile_dst: int32 [32, 128], P(('row', 'col')), may hold values from 0 to 3
- tile_src: int32 [32, 128], P(('row', 'col')), may hold values from 0 to 9
Outputs:
- activations: bfloat16 [8192, 256], P(('row', 'col'))
- grad_features: bfloat16 [8192, 128], P(('row', 'col'))
- grad_weight: float32 [128, 256], replicated
- grad_bias: float32 [256], replicated
Inputs may be any that keep to these rules, and one draw needn't show every extreme that they name: Slots from tile_count on are ignored; some device holds 128 live slots.
All inputs are finite; a program needn't handle non-finite values.
Results may differ from a plain program's by a relative error of at most 0.019.
Values may be sent and summed in bfloat16 or wider, within the bound.
A program may use at most 64 MiB of HBM per device.

v0:
```python
import math
import jax
import jax.numpy as jnp
from jax import lax
from jax.sharding import PartitionSpec as P


def shifted(value, axis, steps):
    count = lax.axis_size(axis)
    pairs = [(source, (source + steps) % count) for source in range(count)]
    return lax.ppermute(value, axis, pairs)


def local(features, weight, bias, grad_out, tiles, tile_count, tile_dst, tile_src):
    node_dev = features.shape[0]
    in_width = features.shape[1]
    tile = tiles.shape[2]
    maxt = tiles.shape[1]
    band = 2
    tiles_dev = node_dev // tile
    n_col = lax.axis_size("col")
    dst_tiles = n_col * tiles_dev
    window_tiles = (2 * band + 1) * tiles_dev
    nodes_all = node_dev * lax.axis_size("row") * n_col
    group = math.gcd(16, maxt)
    pieces = {0: features}
    for offset in (-2, -1, 1, 2):
        pieces[offset] = shifted(features, "row", -offset)
    window = jnp.concatenate([pieces[o] for o in range(-band, band + 1)], 0).reshape(
        window_tiles, tile, in_width
    )
    tile_local = tiles[0]
    count = tile_count[0]
    dst_local = tile_dst[0]
    src_local = tile_src[0]
    turns = (count + group - 1) // group
    offsets_in = jnp.arange(group, dtype=jnp.int32)

    def forward_step(index, acc):
        start = index * group
        tile_block = lax.dynamic_slice_in_dim(tile_local, start, group, 0)
        src_block = lax.dynamic_slice_in_dim(src_local, start, group, 0)
        dst_block = lax.dynamic_slice_in_dim(dst_local, start, group, 0)
        live = (start + offsets_in < count).astype(jnp.float32)
        prod = jnp.einsum(
            "kij,kjh->kih", tile_block, window[src_block], preferred_element_type=jnp.float32
        )
        return acc.at[dst_block].add(prod * live[:, None, None])

    acc = lax.fori_loop(0, turns, forward_step, jnp.zeros((dst_tiles, tile, in_width), jnp.float32))
    summed = lax.psum_scatter(
        acc.reshape(dst_tiles * tile, in_width).astype(jnp.bfloat16),
        "col",
        scatter_dimension=0,
        tiled=True,
    )
    pre = jnp.dot(summed, weight, preferred_element_type=jnp.float32) + bias
    sig = jax.nn.sigmoid(pre)
    activations = (pre * sig).astype(jnp.bfloat16)
    dpre = (grad_out.astype(jnp.float32) * sig * (1.0 + pre * (1.0 - sig))).astype(jnp.bfloat16)
    grad_agg = lax.dot_general(
        dpre, weight, (((1,), (1,)), ((), ())), preferred_element_type=jnp.float32
    ).astype(jnp.bfloat16)
    block_grads = lax.all_gather(grad_agg, "col", axis=0, tiled=True).reshape(
        dst_tiles, tile, in_width
    )

    def back_step(index, acc_back):
        start = index * group
        tile_block = lax.dynamic_slice_in_dim(tile_local, start, group, 0)
        src_block = lax.dynamic_slice_in_dim(src_local, start, group, 0)
        dst_block = lax.dynamic_slice_in_dim(dst_local, start, group, 0)
        live = (start + offsets_in < count).astype(jnp.float32)
        contrib = jnp.einsum(
            "kji,kjh->kih", tile_block, block_grads[dst_block], preferred_element_type=jnp.float32
        )
        return acc_back.at[src_block].add(contrib * live[:, None, None])

    backs = lax.fori_loop(
        0, turns, back_step, jnp.zeros((window_tiles, tile, in_width), jnp.float32)
    )
    backs = backs.reshape(2 * band + 1, node_dev, in_width)
    total = backs[band]
    for offset in (-2, -1, 1, 2):
        total = total + shifted(backs[offset + band], "row", offset)
    grad_features = total.astype(jnp.bfloat16)
    weight_term = lax.dot_general(
        summed, dpre, (((0,), (0,)), ((), ())), preferred_element_type=jnp.float32
    )
    bias_term = jnp.sum(dpre.astype(jnp.float32), 0)
    weight_total, bias_total = lax.psum((weight_term, bias_term), ("row", "col"))
    scale = math.sqrt(nodes_all)
    grad_weight = weight_total / scale
    grad_bias = bias_total / scale
    return (activations, grad_features, grad_weight, grad_bias)


def solution(mesh):
    in_specs = (
        P(("row", "col"), None),
        P(),
        P(),
        P(("row", "col"), None),
        P(("row", "col"), None, None, None),
        P(("row", "col")),
        P(("row", "col"), None),
        P(("row", "col"), None),
    )
    out_specs = (P(("row", "col"), None), P(("row", "col"), None), P(), P())
    return jax.shard_map(local, mesh=mesh, in_specs=in_specs, out_specs=out_specs, check_vma=False)
```

profile of v0, /device:TPU:0, one launch (start us, length us, event | category | flops | bytes accessed | tf_op | source)
XLA Modules:
  0.0 245.5 jit_solution(1033797611451873253)
XLA Ops:
  7.2 0.0 reduce-scatter.2.cloned.1.call-start
  7.2 3.0 %collective-permute-start = (bf16[256,128]{1,0:T(8,128)(2,1)}, bf16[256,128]{1,0:T(8,128)(2,1)S(1)}, u32[]{:S(2)}, u32[]{:S(2)}) collective-permute-start(bf16[256,128]{1,0:T(8,128)(2,1)} %param.12), channel_id=1, source_target_pairs={{0,4},{2,6},{4,8},{6,10},{8,12},{10,14},{12,16},{14,18},{16,20},{1... | collective-permute-start | bytes 196616 | tf_op jit(solution)/shard_map/ppermute | solution.py:11
  10.3 4.1 %collective-permute-start.2 = (bf16[256,128]{1,0:T(8,128)(2,1)}, bf16[256,128]{1,0:T(8,128)(2,1)S(1)}, u32[]{:S(2)}, u32[]{:S(2)}) collective-permute-start(bf16[256,128]{1,0:T(8,128)(2,1)} %param.12), channel_id=1, source_target_pairs={{0,30},{2,0},{4,2},{6,4},{8,6},{10,8},{12,10},{14,12},{16,14},{18,... | collective-permute-start | bytes 196616 | tf_op jit(solution)/shard_map/ppermute | solution.py:11
  14.4 1.9 collective-permute-start.3
  17.0 5.5 %collective-permute-done.1 = bf16[256,128]{1,0:T(8,128)(2,1)S(1)} collective-permute-done((bf16[256,128]{1,0:T(8,128)(2,1)}, bf16[256,128]{1,0:T(8,128)(2,1)S(1)}, u32[]{:S(2)}, u32[]{:S(2)}) %collective-permute-start.1) | collective-permute-done | bytes 65568 | tf_op jit(solution)/shard_map/ppermute | solution.py:11
  22.5 0.9 constant_dynamic-update-slice_fusion.2
  23.4 20.2 %while.22 = (s32[]{:T(128)}, f32[4,128,128]{2,1,0:T(8,128)S(1)}, s32[]{:T(128)}, s32[128]{0:T(128)}, bf16[128,128,128]{2,1,0:T(8,128)(2,1)}, /*index=5*/s32[128]...) while((s32[]{:T(128)}, f32[4,128,128]{2,1,0:T(8,128)S(1)}, ...), condition=%wide.region_2.3_spmd.clone, body=%wide.region_0.2_spmd.clone.sunk | while | flops 67634328 | bytes 6296307 | solution.py:50
  23.5 0.7 compare_convert_fusion.4
  24.1 0.8 compare_select_fusion.6
  24.9 0.6 gather_fusion
  25.5 1.3 convolution_multiply_fusion.4
  26.9 1.6 scatter_fusion
  28.5 0.7 compare_convert_fusion.4
  29.2 0.8 compare_select_fusion.6
  29.9 0.6 gather_fusion
  30.6 1.3 convolution_multiply_fusion.4
  31.9 1.6 scatter_fusion
  33.6 0.7 compare_convert_fusion.4
  34.2 0.8 compare_select_fusion.6
  35.0 0.6 gather_fusion
  35.6 1.3 convolution_multiply_fusion.4
  37.0 1.6 scatter_fusion
  38.6 0.7 compare_convert_fusion.4
  39.3 0.8 compare_select_fusion.6
  40.0 0.6 gather_fusion
  40.7 1.3 convolution_multiply_fusion.4
  42.0 1.6 scatter_fusion
  43.6 0.7 convert_element_type.38
  44.3 0.0 reduce-scatter.2.cloned.1.call-update
  44.3 0.0 all-reduce.2.cloned.1.call-start
  44.4 6.4 %copy.12 = bf16[1,128,128,128]{2,3,1,0:T(8,128)(2,1)} copy(bf16[1,128,128,128]{3,2,1,0:T(8,128)(2,1)} %bitcast.38) | data formatting | bytes 8388608 | tf_op args[4]
  50.9 16.9 %reduce-scatter.2.cloned.1.call-done = bf16[256,128]{1,0:T(8,128)(2,1)} async-done(((bf16[512,128]{1,0:T(8,128)(2,1)}), bf16[256,128]{1,0:T(8,128)(2,1)}) %reduce-scatter.2.cloned.1.call-update) | async-done | bytes 65552 | tf_op jit(solution)/shard_map/reduce_scatter | solution.py:51
  67.8 1.8 convert_reduce_fusion
  69.5 40.4 %psum.15 = f32[256]{0:T(256)S(1)} all-reduce(f32[256]{0:T(256)S(1)} %get-tuple-element.180), channel_id=1, replica_groups=mesh['row'=16,'col'=2] {'row','col'}, use_global_device_ids=true, to_apply=%region_9.10 | all-reduce | flops 256 | bytes 2048 | tf_op jit(solution)/shard_map/psum | solution.py:91
  109.9 0.2 convolution_convert_fusion
  110.1 1.7 fusion.13
  111.8 1.9 all_gather.3
  113.8 17.5 %while.23 = (s32[]{:T(128)}, f32[10,128,128]{2,1,0:T(8,128)S(1)}, s32[]{:T(128)}, s32[128]{0:T(128)S(1)}, bf16[128,128,128]{1,2,0:T(8,128)(2,1)}, /*index=5*/s32...) while((s32[]{:T(128)}, f32[10,128,128]{2,1,0:T(8,128)S(1)}, ...), condition=%wide.region_6.7_spmd.clone, body=%wide.region_4.6_spmd.clone.sunk | while | flops 67634328 | bytes 6296307 | solution.py:79
  113.8 0.7 compare_convert_fusion.5
  114.5 0.1 compare_select_fusion.7
  114.6 0.6 gather_fusion.1
  115.2 1.3 convolution_multiply_fusion.5
  116.6 1.6 scatter_fusion.1
  118.2 0.7 compare_convert_fusion.5
  118.8 0.1 compare_select_fusion.7
  118.9 0.6 gather_fusion.1
  119.6 1.3 convolution_multiply_fusion.5
  120.9 1.6 scatter_fusion.1
  122.6 0.7 compare_convert_fusion.5
  123.2 0.1 compare_select_fusion.7
  123.3 0.6 gather_fusion.1
  124.0 1.3 convolution_multiply_fusion.5
  125.3 1.6 scatter_fusion.1
  127.0 0.7 compare_convert_fusion.5
  127.6 0.1 compare_select_fusion.7
  127.7 0.6 gather_fusion.1
  128.4 1.3 convolution_multiply_fusion.5
  129.7 1.6 scatter_fusion.1
  131.4 0.6 broadcast_multiply_fusion.1
  131.9 5.6 %collective-permute-start.5 = (f32[256,128]{1,0:T(8,128)S(1)}, f32[256,128]{1,0:T(8,128)S(1)}, u32[]{:S(2)}, u32[]{:S(2)}) collective-permute-start(f32[256,128]{1,0:T(8,128)S(1)} %bitcast.43), channel_id=1, source_target_pairs={{0,30},{2,0},{4,2},{6,4},{8,6},{10,8},{12,10},{14,12},{16,14},{18,... | collective-permute-start | bytes 393224 | tf_op jit(solution)/shard_map/ppermute | solution.py:11
  137.6 17.3 %collective-permute-start.4 = (f32[256,128]{1,0:T(8,128)S(1)}, f32[256,128]{1,0:T(8,128)S(1)}, u32[]{:S(2)}, u32[]{:S(2)}) collective-permute-start(f32[256,128]{1,0:T(8,128)S(1)} %bitcast.42), channel_id=1, source_target_pairs={{0,28},{2,30},{4,0},{6,2},{8,4},{10,6},{12,8},{14,10},{16,12},{18,... | collective-permute-start | bytes 393224 | tf_op jit(solution)/shard_map/ppermute | solution.py:11
  154.9 81.5 %all-reduce.2.cloned.1.call-done = f32[128,256]{1,0:T(8,128)} async-done(((f32[128,256]{1,0:T(8,128)}), f32[128,256]{1,0:T(8,128)}) %all-reduce.2.cloned.1.call-update) | async-done | bytes 131088 | tf_op jit(solution)/shard_map/psum | solution.py:91
  236.4 1.6 broadcast_multiply_fusion
  238.0 0.7 fusion.11
  (36 shorter events, 0.3 us)
Async XLA Ops:
  7.2 60.6 %copy-start = (bf16[128,256]{1,0:T(8,128)(2,1)S(1)}, bf16[128,256]{1,0:T(8,128)(2,1)}, u32[]{:S(2)}) copy-start(bf16[128,256]{1,0:T(8,128)(2,1)} %param.13) | copy-start | bytes 196612
  7.2 60.6 %reduce-scatter.2.cloned.1.call-start = ((), (), s32[]{:S(2)}) async-start(), calls=%async_computation.1 | async-start | bytes 196608 | tf_op jit(solution)/shard_map/reduce_scatter | solution.py:51
  7.2 9.7 %collective-permute-start = (bf16[256,128]{1,0:T(8,128)(2,1)}, bf16[256,128]{1,0:T(8,128)(2,1)S(1)}, u32[]{:S(2)}, u32[]{:S(2)}) collective-permute-start(bf16[256,128]{1,0:T(8,128)(2,1)} %param.12), channel_id=1, source_target_pairs={{0,4},{2,6},{4,8},{6,10},{8,12},{10,14},{12,16},{14,18},{16,20},{1... | collective-permute-start | bytes 196616 | tf_op jit(solution)/shard_map/ppermute | solution.py:11
  10.3 13.1 %collective-permute-start.2 = (bf16[256,128]{1,0:T(8,128)(2,1)}, bf16[256,128]{1,0:T(8,128)(2,1)S(1)}, u32[]{:S(2)}, u32[]{:S(2)}) collective-permute-start(bf16[256,128]{1,0:T(8,128)(2,1)} %param.12), channel_id=1, source_target_pairs={{0,30},{2,0},{4,2},{6,4},{8,6},{10,8},{12,10},{14,12},{16,14},{18,... | collective-permute-start | bytes 196616 | tf_op jit(solution)/shard_map/ppermute | solution.py:11
  14.4 8.1 %collective-permute-start.1 = (bf16[256,128]{1,0:T(8,128)(2,1)}, bf16[256,128]{1,0:T(8,128)(2,1)S(1)}, u32[]{:S(2)}, u32[]{:S(2)}) collective-permute-start(bf16[256,128]{1,0:T(8,128)(2,1)} %param.12), channel_id=1, source_target_pairs={{0,2},{2,4},{4,6},{6,8},{8,10},{10,12},{12,14},{14,16},{16,18},{18... | collective-permute-start | bytes 196616 | tf_op jit(solution)/shard_map/ppermute | solution.py:11
  14.4 9.0 %collective-permute-start.3 = (bf16[256,128]{1,0:T(8,128)(2,1)}, bf16[256,128]{1,0:T(8,128)(2,1)S(1)}, u32[]{:S(2)}, u32[]{:S(2)}) collective-permute-start(bf16[256,128]{1,0:T(8,128)(2,1)} %param.12), channel_id=1, source_target_pairs={{0,28},{2,30},{4,0},{6,2},{8,4},{10,6},{12,8},{14,10},{16,12},{18,... | collective-permute-start | bytes 196616 | tf_op jit(solution)/shard_map/ppermute | solution.py:11
  44.3 192.0 %all-reduce.2.cloned.1.call-start = ((), (), s32[]{:S(2)}) async-start(), calls=%async_computation.2 | async-start | bytes 262144 | tf_op jit(solution)/shard_map/psum | solution.py:91
  44.4 23.4 %copy-start.3 = (bf16[256,256]{1,0:T(8,128)(2,1)S(1)}, bf16[256,256]{1,0:T(8,128)(2,1)}, u32[]{:S(2)}) copy-start(bf16[256,256]{1,0:T(8,128)(2,1)} %param.15) | copy-start | bytes 393220
  44.4 23.3 %copy-start.4 = (f32[256]{0:T(256)S(1)}, f32[256]{0:T(256)}, u32[]{:S(2)}) copy-start(f32[256]{0:T(256)} %param.14) | copy-start | bytes 3076
  44.4 69.3 %copy-start.1 = (s32[128]{0:T(128)S(1)}, s32[128]{0:T(128)}, u32[]{:S(2)}) copy-start(s32[128]{0:T(128)} %get-tuple-element.397) | copy-start | bytes 1540
  44.4 69.3 %copy-start.2 = (s32[128]{0:T(128)S(1)}, s32[128]{0:T(128)}, u32[]{:S(2)}) copy-start(s32[128]{0:T(128)} %get-tuple-element.398) | copy-start | bytes 1540
  131.9 106.0 %collective-permute-start.6 = (f32[256,128]{1,0:T(8,128)S(1)}, f32[256,128]{1,0:T(8,128)S(1)}, u32[]{:S(2)}, u32[]{:S(2)}) collective-permute-start(f32[256,128]{1,0:T(8,128)S(1)} %bitcast.44), channel_id=1, source_target_pairs={{0,2},{2,4},{4,6},{6,8},{8,10},{10,12},{12,14},{14,16},{16,18},{18... | collective-permute-start | bytes 393224 | tf_op jit(solution)/shard_map/ppermute | solution.py:11
  131.9 106.0 %collective-permute-start.5 = (f32[256,128]{1,0:T(8,128)S(1)}, f32[256,128]{1,0:T(8,128)S(1)}, u32[]{:S(2)}, u32[]{:S(2)}) collective-permute-start(f32[256,128]{1,0:T(8,128)S(1)} %bitcast.43), channel_id=1, source_target_pairs={{0,30},{2,0},{4,2},{6,4},{8,6},{10,8},{12,10},{14,12},{16,14},{18,... | collective-permute-start | bytes 393224 | tf_op jit(solution)/shard_map/ppermute | solution.py:11
  137.6 100.4 %collective-permute-start.4 = (f32[256,128]{1,0:T(8,128)S(1)}, f32[256,128]{1,0:T(8,128)S(1)}, u32[]{:S(2)}, u32[]{:S(2)}) collective-permute-start(f32[256,128]{1,0:T(8,128)S(1)} %bitcast.42), channel_id=1, source_target_pairs={{0,28},{2,30},{4,0},{6,2},{8,4},{10,6},{12,8},{14,10},{16,12},{18,... | collective-permute-start | bytes 393224 | tf_op jit(solution)/shard_map/ppermute | solution.py:11
  154.9 83.1 %collective-permute-start.7 = (f32[256,128]{1,0:T(8,128)S(1)}, f32[256,128]{1,0:T(8,128)S(1)}, u32[]{:S(2)}, u32[]{:S(2)}) collective-permute-start(f32[256,128]{1,0:T(8,128)S(1)} %bitcast.41), channel_id=1, source_target_pairs={{0,4},{2,6},{4,8},{6,10},{8,12},{10,14},{12,16},{14,18},{16,20},{1... | collective-permute-start | bytes 393224 | tf_op jit(solution)/shard_map/ppermute | solution.py:11
Sparse Core Ops, SparseCore 0:
  44.5 23.2 reduce-scatter.1
  111.9 124.4 all-reduce.1
where the time goes:
time: 247 us; the launch traced here: 245 us
  waiting for transfers between devices  104 us (42%)
  blocking collectives  42.3 us (17%)
  starting transfers between devices  32 us (13%)
  other arithmetic  24.9 us (10%)
  between operations  14.9 us (6%)
  matrix products  14.4 us (6%)
  local copies, waits for them, and re-layouts  12.6 us (5%)
    psum x1, waiting for transfers between devices, local(): lax.psum((weight_term, bias_term), ('row', 'col'))  81.5 us
    psum x1, blocking collectives, local(): lax.psum((weight_term, bias_term), ('row', 'col'))  40.4 us
    ppermute x8, starting transfers between devices, shifted(): return lax.ppermute(value, axis, pairs)  32 us
    reduce_scatter x1, waiting for transfers between devices, local(): lax.psum_scatter(acc.reshape(dst_tiles * tile, in_width).astype(jnp.bfloa...  16.9 us
    unnamed x15, local copies, waits for them, and re-layouts  7.34 us
    scatter-add x4, other arithmetic, back_step(): return acc_back.at[src_block].add(contrib * live[:, None, None])  6.41 us
    scatter-add x4, other arithmetic, forward_step(): return acc.at[dst_block].add(prod * live[:, None, None])  6.4 us
    ppermute x8, waiting for transfers between devices, shifted(): return lax.ppermute(value, axis, pairs)  5.53 us
  transfers between devices with their start and end apart: 10, of which 3 were waited for; matrix products, arithmetic and copies ran while one was open for 11% of the time, Pallas kernels for 0%

commit v1 on v0

--- a/solution.py
+++ b/solution.py
@@ -1,8 +1,17 @@
+import functools
 import math
 import jax
 import jax.numpy as jnp
 from jax import lax
 from jax.sharding import PartitionSpec as P
+
+
+def replace_targets_for(xs, link_axis, a_name):
+    part_next = lax.psum(lax.psum(xs, link_axis), a_name)
+    return part_next
+
+
+number_panel_all = functools.partial(replace_targets_for, link_axis="col", a_name="row")
 
 
 def shifted(value, axis, steps):
@@ -88,7 +97,7 @@
         summed, dpre, (((0,), (0,)), ((), ())), preferred_element_type=jnp.float32
     )
     bias_term = jnp.sum(dpre.astype(jnp.float32), 0)
-    weight_total, bias_total = lax.psum((weight_term, bias_term), ("row", "col"))
+    weight_total, bias_total = number_panel_all((weight_term, bias_term))
     scale = math.sqrt(nodes_all)
     grad_weight = weight_total / scale
     grad_bias = bias_total / scale

time: 247 us -> 269 us (1.089)
  waiting for transfers between devices: 104 us -> 130 us
  starting transfers between devices: 32 us -> 24.4 us
  blocking collectives: 42.3 us -> 46.3 us
    psum x1 -> x2, waiting for transfers between devices: 81.5 us -> 100 us  [replace_targets_for(): part_next = lax.psum(lax.psum(xs, link_axis), a_name)]
    ppermute x8, starting transfers between devices: 32 us -> 24.3 us  [shifted(): return lax.ppermute(value, axis, pairs)]
    ppermute x8, waiting for transfers between devices: 5.53 us -> 12.6 us  [shifted(): return lax.ppermute(value, axis, pairs)]
    psum x1 -> x2, blocking collectives: 40.4 us -> 44.4 us  [replace_targets_for(): part_next = lax.psum(lax.psum(xs, link_axis), a_name)]
  transfers between devices with their start and end apart: 10 -> 11, of which waited for: 3 -> 5; matrix products, arithmetic and copies ran while one was open for 11% -> 10% of each run, Pallas kernels for 0% -> 0%
where the time goes in v1:
time: 269 us; the launch traced here: 267 us
  waiting for transfers between devices  130 us (48%)
  blocking collectives  46.3 us (17%)
  other arithmetic  24.9 us (9%)
  starting transfers between devices  24.4 us (9%)
  between operations  14.6 us (5%)
  matrix products  14.4 us (5%)
  local copies, waits for them, and re-layouts  12.6 us (5%)
    psum x2, waiting for transfers between devices, replace_targets_for(): part_next = lax.psum(lax.psum(xs, link_axis), a_name)  100 us
    psum x2, blocking collectives, replace_targets_for(): part_next = lax.psum(lax.psum(xs, link_axis), a_name)  44.4 us
    ppermute x8, starting transfers between devices, shifted(): return lax.ppermute(value, axis, pairs)  24.3 us
    reduce_scatter x1, waiting for transfers between devices, local(): lax.psum_scatter(acc.reshape(dst_tiles * tile, in_width).astype(jnp.bfloa...  16.9 us
    ppermute x8, waiting for transfers between devices, shifted(): return lax.ppermute(value, axis, pairs)  12.6 us
    unnamed x15, local copies, waits for them, and re-layouts  7.34 us
    scatter-add x4, other arithmetic, back_step(): return acc_back.at[src_block].add(contrib * live[:, None, None])  6.41 us
    scatter-add x4, other arithmetic, forward_step(): return acc.at[dst_block].add(prod * live[:, None, None])  6.4 us
  transfers between devices with their start and end apart: 11, of which 5 were waited for; matrix products, arithmetic and copies ran while one was open for 10% of the time, Pallas kernels for 0%

profile of v1, /device:TPU:0, one launch (start us, length us, event | category | flops | bytes accessed | tf_op | source)
XLA Modules:
  0.0 267.2 jit_solution(3852199006569773221)
XLA Ops:
  7.2 3.0 %collective-permute-start = (bf16[256,128]{1,0:T(8,128)(2,1)}, bf16[256,128]{1,0:T(8,128)(2,1)S(1)}, u32[]{:S(2)}, u32[]{:S(2)}) collective-permute-start(bf16[256,128]{1,0:T(8,128)(2,1)} %param.12), channel_id=1, source_target_pairs={{0,4},{2,6},{4,8},{6,10},{8,12},{10,14},{12,16},{14,18},{16,20},{1... | collective-permute-start | bytes 196616 | tf_op jit(solution)/shard_map/ppermute | solution.py:20
  10.3 4.1 %collective-permute-start.2 = (bf16[256,128]{1,0:T(8,128)(2,1)}, bf16[256,128]{1,0:T(8,128)(2,1)S(1)}, u32[]{:S(2)}, u32[]{:S(2)}) collective-permute-start(bf16[256,128]{1,0:T(8,128)(2,1)} %param.12), channel_id=1, source_target_pairs={{0,30},{2,0},{4,2},{6,4},{8,6},{10,8},{12,10},{14,12},{16,14},{18,... | collective-permute-start | bytes 196616 | tf_op jit(solution)/shard_map/ppermute | solution.py:20
  14.4 1.9 collective-permute-start.3
  17.0 5.5 %collective-permute-done.1 = bf16[256,128]{1,0:T(8,128)(2,1)S(1)} collective-permute-done((bf16[256,128]{1,0:T(8,128)(2,1)}, bf16[256,128]{1,0:T(8,128)(2,1)S(1)}, u32[]{:S(2)}, u32[]{:S(2)}) %collective-permute-start.1) | collective-permute-done | bytes 65568 | tf_op jit(solution)/shard_map/ppermute | solution.py:20
  22.5 0.9 constant_dynamic-update-slice_fusion.2
  23.4 20.2 %while.22 = (s32[]{:T(128)}, f32[4,128,128]{2,1,0:T(8,128)S(1)}, s32[]{:T(128)}, s32[128]{0:T(128)}, bf16[128,128,128]{2,1,0:T(8,128)(2,1)}, /*index=5*/s32[128]...) while((s32[]{:T(128)}, f32[4,128,128]{2,1,0:T(8,128)S(1)}, ...), condition=%wide.region_2.3_spmd.clone, body=%wide.region_0.2_spmd.clone.sunk | while | flops 67634328 | bytes 6296307 | solution.py:59
  23.5 0.7 compare_convert_fusion.4
  24.1 0.8 compare_select_fusion.6
  24.9 0.6 gather_fusion
  25.5 1.3 convolution_multiply_fusion.4
  26.9 1.6 scatter_fusion
  28.5 0.7 compare_convert_fusion.4
  29.2 0.8 compare_select_fusion.6
  29.9 0.6 gather_fusion
  30.6 1.3 convolution_multiply_fusion.4
  31.9 1.6 scatter_fusion
  33.6 0.7 compare_convert_fusion.4
  34.2 0.8 compare_select_fusion.6
  35.0 0.6 gather_fusion
  35.6 1.3 convolution_multiply_fusion.4
  37.0 1.6 scatter_fusion
  38.6 0.7 compare_convert_fusion.4
  39.3 0.8 compare_select_fusion.6
  40.0 0.6 gather_fusion
  40.7 1.3 convolution_multiply_fusion.4
  42.0 1.6 scatter_fusion
  43.6 0.7 convert_element_type.38
  44.4 6.4 %copy.12 = bf16[1,128,128,128]{2,3,1,0:T(8,128)(2,1)} copy(bf16[1,128,128,128]{3,2,1,0:T(8,128)(2,1)} %bitcast.38) | data formatting | bytes 8388608 | tf_op args[4]
  50.9 16.9 %reduce-scatter.2.cloned.1.call-done = bf16[256,128]{1,0:T(8,128)(2,1)} async-done(((bf16[512,128]{1,0:T(8,128)(2,1)}), bf16[256,128]{1,0:T(8,128)(2,1)}) %reduce-scatter.2.cloned.1.call-update) | async-done | bytes 65552 | tf_op jit(solution)/shard_map/reduce_scatter | solution.py:60
  67.8 1.8 convert_reduce_fusion
  69.5 2.4 psum.30
  72.0 41.9 %psum.31 = f32[256]{0:T(256)S(1)} all-reduce(f32[256]{0:T(256)S(1)} %psum.30), channel_id=1, replica_groups=mesh['row'=16,'col'=2] {'row'}, use_global_device_ids=true, to_apply=%region_11.12 | all-reduce | flops 256 | bytes 2048 | tf_op jit(solution)/shard_map/psum | solution.py:10
  113.9 0.2 convolution_convert_fusion
  114.1 1.7 fusion.13
  115.8 1.9 all_gather.3
  117.8 17.5 %while.23 = (s32[]{:T(128)}, f32[10,128,128]{2,1,0:T(8,128)S(1)}, s32[]{:T(128)}, s32[128]{0:T(128)S(1)}, bf16[128,128,128]{1,2,0:T(8,128)(2,1)}, /*index=5*/s32...) while((s32[]{:T(128)}, f32[10,128,128]{2,1,0:T(8,128)S(1)}, ...), condition=%wide.region_6.7_spmd.clone, body=%wide.region_4.6_spmd.clone.sunk | while | flops 67634328 | bytes 6296307 | solution.py:88
  117.8 0.7 compare_convert_fusion.5
  118.5 0.1 compare_select_fusion.7
  118.6 0.6 gather_fusion.1
  119.2 1.3 convolution_multiply_fusion.5
  120.6 1.6 scatter_fusion.1
  122.2 0.7 compare_convert_fusion.5
  122.9 0.1 compare_select_fusion.7
  123.0 0.6 gather_fusion.1
  123.6 1.3 convolution_multiply_fusion.5
  125.0 1.6 scatter_fusion.1
  126.6 0.7 compare_convert_fusion.5
  127.3 0.1 compare_select_fusion.7
  127.4 0.6 gather_fusion.1
  128.0 1.3 convolution_multiply_fusion.5
  129.4 1.6 scatter_fusion.1
  131.0 0.7 compare_convert_fusion.5
  131.6 0.1 compare_select_fusion.7
  131.7 0.6 gather_fusion.1
  132.4 1.3 convolution_multiply_fusion.5
  133.7 1.6 scatter_fusion.1
  135.5 5.6 %collective-permute-start.5 = (f32[256,128]{1,0:T(8,128)S(1)}, f32[256,128]{1,0:T(8,128)S(1)}, u32[]{:S(2)}, u32[]{:S(2)}) collective-permute-start(f32[256,128]{1,0:T(8,128)S(1)} %bitcast.43), channel_id=1, source_target_pairs={{0,30},{2,0},{4,2},{6,4},{8,6},{10,8},{12,10},{14,12},{16,14},{18,... | collective-permute-start | bytes 393224 | tf_op jit(solution)/shard_map/ppermute | solution.py:20
  141.1 9.6 %collective-permute-start.4 = (f32[256,128]{1,0:T(8,128)S(1)}, f32[256,128]{1,0:T(8,128)S(1)}, u32[]{:S(2)}, u32[]{:S(2)}) collective-permute-start(f32[256,128]{1,0:T(8,128)S(1)} %bitcast.42), channel_id=1, source_target_pairs={{0,28},{2,30},{4,0},{6,2},{8,4},{10,6},{12,8},{14,10},{16,12},{18,... | collective-permute-start | bytes 393224 | tf_op jit(solution)/shard_map/ppermute | solution.py:20
  150.7 0.6 broadcast_multiply_fusion.1
  151.3 1.9 collective-permute-done.4
  153.2 5.1 %collective-permute-done.7 = f32[256,128]{1,0:T(8,128)S(1)} collective-permute-done((f32[256,128]{1,0:T(8,128)S(1)}, f32[256,128]{1,0:T(8,128)S(1)}, u32[]{:S(2)}, u32[]{:S(2)}) %collective-permute-start.7) | collective-permute-done | bytes 131104 | tf_op jit(solution)/shard_map/ppermute | solution.py:20
  158.4 0.7 fusion.11
  159.0 100.1 %all-reduce.5.cloned.1.call-done = f32[128,256]{1,0:T(8,128)} async-done(((f32[128,256]{1,0:T(8,128)}), f32[128,256]{1,0:T(8,128)}) %all-reduce.5.cloned.1.call-update) | async-done | bytes 131088 | tf_op jit(solution)/shard_map/psum | solution.py:10
  259.1 1.6 broadcast_multiply_fusion
  (40 shorter events, 0.5 us)
Async XLA Ops:
  7.2 60.6 %copy-start = (bf16[128,256]{1,0:T(8,128)(2,1)S(1)}, bf16[128,256]{1,0:T(8,128)(2,1)}, u32[]{:S(2)}) copy-start(bf16[128,256]{1,0:T(8,128)(2,1)} %param.13) | copy-start | bytes 196612
  7.2 60.6 %reduce-scatter.2.cloned.1.call-start = ((), (), s32[]{:S(2)}) async-start(), calls=%async_computation.1 | async-start | bytes 196608 | tf_op jit(solution)/shard_map/reduce_scatter | solution.py:60
  7.2 9.7 %collective-permute-start = (bf16[256,128]{1,0:T(8,128)(2,1)}, bf16[256,128]{1,0:T(8,128)(2,1)S(1)}, u32[]{:S(2)}, u32[]{:S(2)}) collective-permute-start(bf16[256,128]{1,0:T(8,128)(2,1)} %param.12), channel_id=1, source_target_pairs={{0,4},{2,6},{4,8},{6,10},{8,12},{10,14},{12,16},{14,18},{16,20},{1... | collective-permute-start | bytes 196616 | tf_op jit(solution)/shard_map/ppermute | solution.py:20
  10.3 13.1 %collective-permute-start.2 = (bf16[256,128]{1,0:T(8,128)(2,1)}, bf16[256,128]{1,0:T(8,128)(2,1)S(1)}, u32[]{:S(2)}, u32[]{:S(2)}) collective-permute-start(bf16[256,128]{1,0:T(8,128)(2,1)} %param.12), channel_id=1, source_target_pairs={{0,30},{2,0},{4,2},{6,4},{8,6},{10,8},{12,10},{14,12},{16,14},{18,... | collective-permute-start | bytes 196616 | tf_op jit(solution)/shard_map/ppermute | solution.py:20
  14.4 8.1 %collective-permute-start.1 = (bf16[256,128]{1,0:T(8,128)(2,1)}, bf16[256,128]{1,0:T(8,128)(2,1)S(1)}, u32[]{:S(2)}, u32[]{:S(2)}) collective-permute-start(bf16[256,128]{1,0:T(8,128)(2,1)} %param.12), channel_id=1, source_target_pairs={{0,2},{2,4},{4,6},{6,8},{8,10},{10,12},{12,14},{14,16},{16,18},{18... | collective-permute-start | bytes 196616 | tf_op jit(solution)/shard_map/ppermute | solution.py:20
  14.4 9.0 %collective-permute-start.3 = (bf16[256,128]{1,0:T(8,128)(2,1)}, bf16[256,128]{1,0:T(8,128)(2,1)S(1)}, u32[]{:S(2)}, u32[]{:S(2)}) collective-permute-start(bf16[256,128]{1,0:T(8,128)(2,1)} %param.12), channel_id=1, source_target_pairs={{0,28},{2,30},{4,0},{6,2},{8,4},{10,6},{12,8},{14,10},{16,12},{18,... | collective-permute-start | bytes 196616 | tf_op jit(solution)/shard_map/ppermute | solution.py:20
  44.3 106.9 %all-reduce.3.cloned.1.call-start = ((), (), s32[]{:S(2)}) async-start(), calls=%async_computation.2 | async-start | bytes 262144 | tf_op jit(solution)/shard_map/psum | solution.py:10
  44.4 23.4 %copy-start.3 = (bf16[256,256]{1,0:T(8,128)(2,1)S(1)}, bf16[256,256]{1,0:T(8,128)(2,1)}, u32[]{:S(2)}) copy-start(bf16[256,256]{1,0:T(8,128)(2,1)} %param.15) | copy-start | bytes 393220
  44.4 23.3 %copy-start.4 = (f32[256]{0:T(256)S(1)}, f32[256]{0:T(256)}, u32[]{:S(2)}) copy-start(f32[256]{0:T(256)} %param.14) | copy-start | bytes 3076
  44.4 73.4 %copy-start.1 = (s32[128]{0:T(128)S(1)}, s32[128]{0:T(128)}, u32[]{:S(2)}) copy-start(s32[128]{0:T(128)} %get-tuple-element.401) | copy-start | bytes 1540
  44.4 73.4 %copy-start.2 = (s32[128]{0:T(128)S(1)}, s32[128]{0:T(128)}, u32[]{:S(2)}) copy-start(s32[128]{0:T(128)} %get-tuple-element.402) | copy-start | bytes 1540
  115.8 143.3 %all-reduce.5.cloned.1.call-start = ((), (), s32[]{:S(2)}) async-start(), calls=%async_computation.3 | async-start | bytes 262144 | tf_op jit(solution)/shard_map/psum | solution.py:10
  135.4 15.9 %collective-permute-start.6 = (f32[256,128]{1,0:T(8,128)S(1)}, f32[256,128]{1,0:T(8,128)S(1)}, u32[]{:S(2)}, u32[]{:S(2)}) collective-permute-start(f32[256,128]{1,0:T(8,128)S(1)} %bitcast.44), channel_id=1, source_target_pairs={{0,2},{2,4},{4,6},{6,8},{8,10},{10,12},{12,14},{14,16},{16,18},{18... | collective-permute-start | bytes 393224 | tf_op jit(solution)/shard_map/ppermute | solution.py:20
  135.5 15.8 %collective-permute-start.5 = (f32[256,128]{1,0:T(8,128)S(1)}, f32[256,128]{1,0:T(8,128)S(1)}, u32[]{:S(2)}, u32[]{:S(2)}) collective-permute-start(f32[256,128]{1,0:T(8,128)S(1)} %bitcast.43), channel_id=1, source_target_pairs={{0,30},{2,0},{4,2},{6,4},{8,6},{10,8},{12,10},{14,12},{16,14},{18,... | collective-permute-start | bytes 393224 | tf_op jit(solution)/shard_map/ppermute | solution.py:20
  141.1 12.1 %collective-permute-start.4 = (f32[256,128]{1,0:T(8,128)S(1)}, f32[256,128]{1,0:T(8,128)S(1)}, u32[]{:S(2)}, u32[]{:S(2)}) collective-permute-start(f32[256,128]{1,0:T(8,128)S(1)} %bitcast.42), channel_id=1, source_target_pairs={{0,28},{2,30},{4,0},{6,2},{8,4},{10,6},{12,8},{14,10},{16,12},{18,... | collective-permute-start | bytes 393224 | tf_op jit(solution)/shard_map/ppermute | solution.py:20
  150.7 7.7 %collective-permute-start.7 = (f32[256,128]{1,0:T(8,128)S(1)}, f32[256,128]{1,0:T(8,128)S(1)}, u32[]{:S(2)}, u32[]{:S(2)}) collective-permute-start(f32[256,128]{1,0:T(8,128)S(1)} %bitcast.41), channel_id=1, source_target_pairs={{0,4},{2,6},{4,8},{6,10},{8,12},{10,14},{12,16},{14,18},{16,20},{1... | collective-permute-start | bytes 393224 | tf_op jit(solution)/shard_map/ppermute | solution.py:20
Sparse Core Ops, SparseCore 0:
  44.5 23.2 reduce-scatter.1
  115.9 13.7 all-reduce.2
  151.4 107.6 all-reduce.4
